TPU v7x, 32 devices: a whole 2x2x4 slice. The times are simulated.
32 devices in a mesh: pts: 32 (over z, y, x, core).
Axes of the slice: x: 2, y: 2, z: 4, core: 2. Of those that a mesh axis runs over, the one named last changes fastest.
Arguments:
- features: float32 [65536, 128], P('pts'), may hold values from -6 to 6
- factor: float32 [65536, 1024], P('pts'), may hold values from -0.375 to 0.375
- targets: float32 [65536, 256], P('pts'), may hold values from -6 to 6
- pivots: int32 [4, 256], replicated, may hold values from 0 to 65535, as said below
Outputs:
- residuals: float32 [65536, 256], P('pts')
- scores: float32 [4, 256, 256], replicated
Inputs may be any that keep to these rules, and one draw needn't show every extreme that they name: Owners of pivots are uneven: low point indices are picked more often. Indices may repeat.
All inputs are finite; a program needn't handle non-finite values.
Results may differ from a plain program's by a relative error of at most 0.0003.
Values sent between devices are 32-bit elements; how exact they have to be, the bound alone decides.
A program may use at most 192 MiB of HBM per device.

v0:
```python
import jax
import jax.numpy as jnp
from jax import lax
from jax.sharding import PartitionSpec as P

FEATS = 128
PIV = 256
BLOCKS = 4


def hdot(a, b):
    return jnp.dot(a, b, precision=lax.Precision.HIGHEST, preferred_element_type=jnp.float32)


def kernel_cols(points, pivot_feats):
    left = jnp.sum(points * points, axis=1)[:, None]
    right = jnp.sum(pivot_feats * pivot_feats, axis=1)[None, :]
    cross = hdot(points, pivot_feats.T)
    return jnp.exp(-(left + right - 2.0 * cross) * (0.5 / FEATS))


def owned_rows(table, index_list, offset, count):
    local = index_list - offset
    owned = (local >= 0) & (local < count)
    safe = jnp.clip(local, 0, count - 1)
    return jnp.take(table, safe, axis=0) * owned[:, None].astype(table.dtype)


def per_device(features, factor, targets, pivots):
    count = features.shape[0]
    npts = count * lax.axis_size("pts")
    offset = lax.axis_index("pts") * count
    eye = jnp.eye(PIV, dtype=jnp.float32)
    resid = targets
    extras = []
    score_list = []
    for block in range(BLOCKS):
        idx = pivots[block]
        if block > 0:
            joined = jnp.concatenate(extras, axis=1)
        if block > 0:
            extra_part = owned_rows(joined, idx, offset, count)
        else:
            extra_part = jnp.zeros((PIV, 8), jnp.float32)
        piv_feats, piv_rows, piv_extra = lax.psum(
            (
                owned_rows(features, idx, offset, count),
                owned_rows(factor, idx, offset, count),
                extra_part,
            ),
            "pts",
        )
        cols = kernel_cols(features, piv_feats) - hdot(factor, piv_rows.T)
        if block > 0:
            cols = cols - hdot(joined, piv_extra.T)
        gram = lax.psum(hdot(cols.T, cols), "pts")
        lower = jnp.linalg.cholesky(gram / npts + 0.05 * eye)
        normed = lax.linalg.triangular_solve(
            lower, cols, left_side=False, lower=True, transpose_a=True
        )
        qq, qy = lax.psum((hdot(normed.T, normed), hdot(normed.T, resid)), "pts")
        scaled_qq = qq / npts
        ridge = jnp.linalg.cholesky(scaled_qq + 0.1 * eye)
        middle = lax.linalg.triangular_solve(ridge, qy / npts, left_side=True, lower=True)
        beta = lax.linalg.triangular_solve(
            ridge, middle, left_side=True, lower=True, transpose_a=True
        )
        resid = resid - hdot(normed, beta)
        score_list.append(qy / jnp.sqrt(jnp.float32(npts)))
        extras.append(normed * (1.0 / jnp.sqrt(jnp.float32(PIV))))
    return (resid, jnp.stack(score_list))


def solution(mesh):
    in_specs = (P("pts", None), P("pts", None), P("pts", None), P())
    out_specs = (P("pts", None), P())
    return jax.shard_map(
        per_device, mesh=mesh, in_specs=in_specs, out_specs=out_specs, check_vma=False
    )
```

profile of v0, /device:TPU:0, one launch (start us, length us, event | category | flops | bytes accessed | tf_op | source)
XLA Modules:
  0.0 1928.4 jit_solution(473149198986484992)
XLA Ops:
  10.2 5.0 gather_fusion.4
  18.0 5.0 gather_fusion.6
  26.0 126.0 %all-reduce.34.cloned.1.call-done = (f32[256,1024]{1,0:T(8,128)}, f32[256,128]{1,0:T(8,128)}) async-done(((f32[256,1024]{1,0:T(8,128)}, f32[256,128]{1,0:T(8,128)}), (f32[256,1024]{1,0:T(8,128)}, f32[256,128]{1,0:T(8,128)})) %all-reduce.34.cloned.1.call-update) | async-done | bytes 1179664 | tf_op jit(solution)/shard_map/psum | solution.py:45
  153.1 10.0 convolution_bitcast_fusion.3
  169.3 122.7 %all-reduce.18.cloned.1.call-done = f32[256,256]{0,1:T(8,128)} async-done(((f32[256,256]{0,1:T(8,128)}), f32[256,256]{0,1:T(8,128)}) %all-reduce.18.cloned.1.call-update) | async-done | bytes 262160 | tf_op jit(solution)/shard_map/psum | solution.py:56
  296.5 11.7 cholesky.382
  308.8 10.4 custom-call.33
  321.4 11.7 cholesky.399
  338.8 5.7 while.24
  345.2 20.5 %custom-call.34 = f32[2,128,128]{1,2,0:T(8,128)S(1)} custom-call(f32[2,128,128]{2,1,0:T(8,128)} %copy-done.72), custom_call_target="InvertDiagBlocksLowerTriangular" | custom-call | tf_op jit(solution)/shard_map/triangular_solve/custom-call.0 | solution.py:58
  376.1 5.9 gather_fusion.8
  385.7 121.8 %all-reduce.32.cloned.1.call-done = (f32[256,1024]{1,0:T(8,128)}, f32[256,128]{1,0:T(8,128)}, f32[256,256]{1,0:T(8,128)}) async-done(((f32[256,1024]{1,0:T(8,128)}, f32[256,128]{1,0:T(8,128)}, f32[256,256]{1,0:T(8,128)}), (f32[256,1024]{1,0:T(8,128)}, f32[256,128]{1,0:T(8,128)}, f32[256,256]{1,0:T(8,128)})) %all-reduce.32.cloned.1.call-update) | async-done | bytes 1441808 | tf_op jit(solution)/shard_map/psum | solution.py:45
  507.4 10.1 convolution_bitcast_fusion.2
  527.6 122.5 %all-reduce.20.cloned.1.call-done = f32[256,256]{0,1:T(8,128)} async-done(((f32[256,256]{0,1:T(8,128)}), f32[256,256]{0,1:T(8,128)}) %all-reduce.20.cloned.1.call-update) | async-done | bytes 262160 | tf_op jit(solution)/shard_map/psum | solution.py:56
  654.7 11.7 cholesky.450
  667.0 9.8 custom-call.38
  679.0 11.7 cholesky.467
  695.0 6.0 while.26
  701.7 20.5 %custom-call.39 = f32[2,128,128]{1,2,0:T(8,128)S(1)} custom-call(f32[2,128,128]{2,1,0:T(8,128)} %copy-done.73), custom_call_target="InvertDiagBlocksLowerTriangular" | custom-call | tf_op jit(solution)/shard_map/triangular_solve/custom-call.0 | solution.py:58
  731.8 5.3 copy.45
  737.1 4.3 gather_fusion.1
  743.6 5.9 gather_fusion.10
  751.7 4.8 fusion.39
  756.5 5.8 fusion.38
  762.3 113.8 %all-reduce.30.cloned.1.call-done = (f32[256,1024]{1,0:T(8,128)}, f32[256,128]{1,0:T(8,128)}, f32[256,512]{1,0:T(8,128)}) async-done(((f32[256,1024]{1,0:T(8,128)}, f32[256,128]{1,0:T(8,128)}, f32[256,512]{1,0:T(8,128)}), (f32[256,1024]{1,0:T(8,128)}, f32[256,128]{1,0:T(8,128)}, f32[256,512]{1,0:T(8,128)})) %all-reduce.30.cloned.1.call-update) | async-done | bytes 1703952 | tf_op jit(solution)/shard_map/psum | solution.py:45
  876.0 10.1 convolution_bitcast_fusion.1
  901.9 123.9 %all-reduce.28.cloned.1.call-done = (f32[256,256]{0,1:T(8,128)}, f32[256,256]{0,1:T(8,128)}, f32[256,256]{0,1:T(8,128)}) async-done(((f32[256,256]{0,1:T(8,128)}, f32[256,256]{0,1:T(8,128)}, f32[256,256]{0,1:T(8,128)}), (f32[256,256]{0,1:T(8,128)}, f32[256,256]{0,1:T(8,128)}, f32[256,256]{0,1:T(8,128)})) %all-reduce.28.cloned.1.call-update) | async-done | bytes 786448 | tf_op jit(solution)/shard_map/psum | solution.py:61
  1030.3 11.7 cholesky.518
  1042.7 9.8 custom-call.43
  1054.7 12.1 cholesky.535
  1071.1 5.1 while.28
  1076.9 20.5 %custom-call.44 = f32[2,128,128]{1,2,0:T(8,128)S(1)} custom-call(f32[2,128,128]{2,1,0:T(8,128)} %copy-done.74), custom_call_target="InvertDiagBlocksLowerTriangular" | custom-call | tf_op jit(solution)/shard_map/triangular_solve/custom-call.0 | solution.py:58
  1107.3 6.7 copy.52
  1114.1 5.2 gather_fusion.2
  1125.7 11.7 cholesky.416
  1137.5 9.8 custom-call.35
  1149.5 11.7 cholesky.433
  1169.5 20.9 %custom-call.37 = f32[2,128,128]{1,2,0:T(8,128)S(1)} custom-call(f32[2,128,128]{2,1,0:T(8,128)} %copy-done.75), custom_call_target="InvertDiagBlocksLowerTriangular" | custom-call | tf_op jit(solution)/shard_map/triangular_solve/custom-call.5 | solution.py:65
  1194.2 5.4 convolution_subtract_fusion.5
  1205.2 4.7 fusion.35
  1209.9 131.8 %all-reduce.26.cloned.1.call-done = (f32[256,256]{0,1:T(8,128)}, f32[256,256]{0,1:T(8,128)}, f32[256,1024]{1,0:T(8,128)}, f32[256,128]{1,0:T(8,128)}, f32[256,768]{1,0:T(8,128)}) async-done(((f32[256,256]{0,1:T(8,128)}, f32[256,256]{0,1:T(8,128)}, f32[256,1024]{1,0:T(8,128)}, f32[256,128]{1,0:T(8,128)}, f32[256,768]{1,0:T(8,128)}), (f32[256,256]{0,1:T(8,128)}, f32[256,256]{0,1:T(8,128)}, ...) | async-done | bytes 2490384 | tf_op jit(solution)/shard_map/psum | solution.py:61
  1341.7 10.2 convolution_bitcast_fusion
  1354.4 5.7 convolution_subtract_fusion
  1363.0 11.9 cholesky.484
  1375.0 9.8 custom-call.40
  1385.3 11.7 cholesky.501
  1403.7 20.1 %custom-call.42 = f32[2,128,128]{1,2,0:T(8,128)S(1)} custom-call(f32[2,128,128]{2,1,0:T(8,128)S(1)} %get-tuple-element.91), custom_call_target="InvertDiagBlocksLowerTriangular" | custom-call | tf_op jit(solution)/shard_map/triangular_solve/custom-call.5 | solution.py:65
  1426.5 5.3 convolution_subtract_fusion.3
  1437.6 128.9 %all-reduce.24.cloned.1.call-done = (f32[256,256]{0,1:T(8,128)}, f32[256,256]{0,1:T(8,128)}, f32[256,256]{0,1:T(8,128)}) async-done(((f32[256,256]{0,1:T(8,128)}, f32[256,256]{0,1:T(8,128)}, f32[256,256]{0,1:T(8,128)}), (f32[256,256]{0,1:T(8,128)}, f32[256,256]{0,1:T(8,128)}, f32[256,256]{0,1:T(8,128)})) %all-reduce.24.cloned.1.call-update) | async-done | bytes 786448 | tf_op jit(solution)/shard_map/psum | solution.py:61
  1571.1 11.7 cholesky.586
  1582.9 9.8 custom-call.48
  1594.8 11.7 cholesky.603
  1614.8 20.9 %custom-call.49 = f32[2,128,128]{1,2,0:T(8,128)S(1)} custom-call(f32[2,128,128]{2,1,0:T(8,128)} %copy-done.76), custom_call_target="InvertDiagBlocksLowerTriangular" | custom-call | tf_op jit(solution)/shard_map/triangular_solve/custom-call.0 | solution.py:58
  1640.2 11.7 cholesky.552
  1652.0 9.8 custom-call.45
  1662.3 11.9 cholesky.569
  1677.1 4.3 while.29
  1682.0 20.5 %custom-call.47 = f32[2,128,128]{1,2,0:T(8,128)S(1)} custom-call(f32[2,128,128]{2,1,0:T(8,128)} %copy-done.77), custom_call_target="InvertDiagBlocksLowerTriangular" | custom-call | tf_op jit(solution)/shard_map/triangular_solve/custom-call.5 | solution.py:65
  1716.8 127.3 %all-reduce.22.cloned.1.call-done = (f32[256,256]{0,1:T(8,128)}, f32[256,256]{0,1:T(8,128)}) async-done(((f32[256,256]{0,1:T(8,128)}, f32[256,256]{0,1:T(8,128)}), (f32[256,256]{0,1:T(8,128)}, f32[256,256]{0,1:T(8,128)})) %all-reduce.22.cloned.1.call-update) | async-done | bytes 524304 | tf_op jit(solution)/shard_map/psum | solution.py:61
  1847.4 11.9 cholesky.620
  1859.4 9.8 custom-call.50
  1870.7 11.7 cholesky.637
  1891.0 20.7 %custom-call.52 = f32[2,128,128]{1,2,0:T(8,128)S(1)} custom-call(f32[2,128,128]{2,1,0:T(8,128)} %copy-done.71), custom_call_target="InvertDiagBlocksLowerTriangular" | custom-call | tf_op jit(solution)/shard_map/triangular_solve/custom-call.5 | solution.py:65
  1915.5 6.0 convolution_subtract_fusion.1
  (457 shorter events, 244.8 us)
Async XLA Ops:
  7.2 144.9 %all-reduce.34.cloned.1.call-start = ((), (), s32[]{:S(2)}) async-start(), calls=%async_computation.8 | async-start | bytes 2359296 | tf_op jit(solution)/shard_map/psum | solution.py:45
  9.3 15.5 copy-start.83
  10.2 14.7 copy-start.78
  10.2 5.1 copy-start
  18.0 274.0 %all-reduce.18.cloned.1.call-start = ((), (), s32[]{:S(2)}) async-start(), calls=%async_computation | async-start | bytes 524288 | tf_op jit(solution)/shard_map/psum | solution.py:56
  153.1 10.0 copy-start.67
  167.8 339.6 %all-reduce.32.cloned.1.call-start = ((), (), s32[]{:S(2)}) async-start(), calls=%async_computation.7 | async-start | bytes 2883584 | tf_op jit(solution)/shard_map/psum | solution.py:45
  333.2 3.2 copy-start.53
  371.8 2.7 copy-start.79
  371.8 2.7 copy-start.84
  371.8 3.6 copy-start.80
  371.8 3.7 copy-start.81
  375.4 274.7 %all-reduce.20.cloned.1.call-start = ((), (), s32[]{:S(2)}) async-start(), calls=%async_computation.1 | async-start | bytes 524288 | tf_op jit(solution)/shard_map/psum | solution.py:56
  383.3 142.9 %copy-start.85 = (pred[256]{0:T(512)(128)(4,1)}, pred[256]{0:T(512)(128)(4,1)S(1)}, u32[]{:S(2)}) copy-start(pred[256]{0:T(512)(128)(4,1)S(1)} %get-tuple-element.278) | copy-start | bytes 772
  507.4 10.1 copy-start.65
  523.3 3.7 copy-start.88
  525.9 350.1 %all-reduce.30.cloned.1.call-start = ((), (), s32[]{:S(2)}) async-start(), calls=%async_computation.6 | async-start | bytes 3407872 | tf_op jit(solution)/shard_map/psum | solution.py:45
  690.7 3.3 copy-start.48
  722.2 2.4 copy-start.12
  737.1 4.3 copy-start.86
  743.5 282.3 %all-reduce.28.cloned.1.call-start = ((), (), s32[]{:S(2)}) async-start(), calls=%async_computation.5 | async-start | bytes 1572864 | tf_op jit(solution)/shard_map/psum | solution.py:61
  743.6 6.7 copy-start.87
  743.6 7.3 copy-start.82
  750.2 6.2 copy-start.7
  750.2 6.2 copy-start.19
  876.0 10.1 copy-start.66
  896.5 445.2 %all-reduce.26.cloned.1.call-start = ((), (), s32[]{:S(2)}) async-start(), calls=%async_computation.4 | async-start | bytes 4980736 | tf_op jit(solution)/shard_map/psum | solution.py:61
  896.8 2.6 copy-start.22
  896.8 2.5 copy-start.39
  1066.8 3.3 copy-start.49
  1097.4 2.4 copy-start.10
  1114.1 7.4 copy-start.43
  1121.5 43.4 %copy-start.90 = (s32[2,2]{1,0:T(2,128)S(1)}, s32[2,2]{1,0:T(2,128)}, u32[]{:S(2)}) copy-start(s32[2,2]{1,0:T(2,128)} %get-tuple-element.749) | copy-start | bytes 52
  1161.2 2.7 copy-start.50
  1190.4 3.8 copy-start.8
  1190.4 3.8 copy-start.20
  1194.2 6.7 copy-start.23
  1194.2 6.7 copy-start.40
  1205.1 361.3 %all-reduce.24.cloned.1.call-start = ((), (), s32[]{:S(2)}) async-start(), calls=%async_computation.3 | async-start | bytes 1572864 | tf_op jit(solution)/shard_map/psum | solution.py:61
  1341.7 10.2 copy-start.68
  1360.2 2.6 copy-start.13
  1360.2 2.6 copy-start.46
  1362.8 61.0 %copy-start.69 = (f32[256,256]{0,1:T(8,128)S(1)}, f32[256,256]{0,1:T(8,128)}, u32[]{:S(2)}) copy-start(f32[256,256]{0,1:T(8,128)} %get-tuple-element.171) | copy-start | bytes 786436
  1399.7 26.8 %copy-start.24 = (f32[128,2048]{1,0:T(8,128)S(1)}, f32[128,2048]{1,0:T(8,128)}, u32[]{:S(2)}) copy-start(f32[128,2048]{1,0:T(8,128)} %copy-done.21) | copy-start | bytes 3145732
  1399.7 26.8 %copy-start.41 = (f32[2048,128]{0,1:T(8,128)S(1)}, f32[2048,128]{0,1:T(8,128)}, u32[]{:S(2)}) copy-start(f32[2048,128]{0,1:T(8,128)} %copy-done.38) | copy-start | bytes 3145732
  1426.5 6.7 copy-start.16
  1426.5 6.7 copy-start.36
  1437.4 406.7 %all-reduce.22.cloned.1.call-start = ((), (), s32[]{:S(2)}) async-start(), calls=%async_computation.2 | async-start | bytes 1048576 | tf_op jit(solution)/shard_map/psum | solution.py:61
  1568.1 67.6 %copy-start.14 = (f32[2048,256]{0,1:T(8,128)S(1)}, f32[2048,256]{0,1:T(8,128)}, u32[]{:S(2)}) copy-start(f32[2048,256]{0,1:T(8,128)} %copy-done.13) | copy-start | bytes 6291460
  1606.6 2.6 copy-start.51
  1636.8 3.2 copy-start.32
  1636.8 3.2 copy-start.44
  1677.0 29.2 %copy-start.26 = (f32[2048,256]{1,0:T(8,128)S(1)}, f32[2048,256]{1,0:T(8,128)}, u32[]{:S(2)}) copy-start(f32[2048,256]{1,0:T(8,128)} %copy-done.25) | copy-start | bytes 6291460
  1702.5 3.7 copy-start.37
  1706.2 3.6 copy-start.33
  1706.3 3.6 copy-start.42
  1709.9 2.6 copy-start.28
  1712.5 133.2 %copy-start.54 = (f32[1,256,256]{1,2,0:T(8,128)S(1)}, f32[1,256,256]{1,2,0:T(8,128)}, u32[]{:S(2)}) copy-start(f32[1,256,256]{1,2,0:T(8,128)} %get-tuple-element.209) | copy-start | bytes 786436
  1712.5 133.2 %copy-start.55 = (f32[1,256,256]{1,2,0:T(8,128)S(1)}, f32[1,256,256]{1,2,0:T(8,128)}, u32[]{:S(2)}) copy-start(f32[1,256,256]{1,2,0:T(8,128)} %get-tuple-element.211) | copy-start | bytes 786436
  1712.5 133.2 %copy-start.56 = (f32[1,256,256]{1,2,0:T(8,128)S(1)}, f32[1,256,256]{1,2,0:T(8,128)}, u32[]{:S(2)}) copy-start(f32[1,256,256]{1,2,0:T(8,128)} %get-tuple-element.213) | copy-start | bytes 786436
  1847.4 21.8 %copy-start.62 = (f32[256,256]{1,0:T(8,128)}, f32[256,256]{1,0:T(8,128)S(1)}, u32[]{:S(2)}) copy-start(f32[256,256]{1,0:T(8,128)S(1)} %fusion.52) | copy-start | bytes 786436
  1869.4 46.0 %copy-start.29 = (f32[2048,256]{1,0:T(8,128)S(1)}, f32[2048,256]{1,0:T(8,128)}, u32[]{:S(2)}) copy-start(f32[2048,256]{1,0:T(8,128)} %copy-done.28) | copy-start | bytes 6291460
  1869.5 46.0 %copy-start.34 = (f32[128,2048]{1,0:T(8,128)S(1)}, f32[128,2048]{1,0:T(8,128)}, u32[]{:S(2)}) copy-start(f32[128,2048]{1,0:T(8,128)} %copy-done.32) | copy-start | bytes 3145732
  1882.5 2.6 copy-start.52
  (36 other events, 51.9 us)
Sparse Core Ops, SparseCore 0:
  18.1 133.8 all-reduce.33
  168.0 123.9 all-reduce.17
  375.6 131.8 all-reduce.31
  526.1 124.0 all-reduce.19
  743.6 132.3 all-reduce.29
  896.6 129.1 all-reduce.27
  1205.3 136.4 all-reduce.25
  1437.5 128.9 all-reduce.23
  1716.9 127.1 all-reduce.21
where the time goes:
time: 1940 us; the launch traced here: 1930 us
  waiting for transfers between devices  1120 us (58%)
  other arithmetic  502 us (26%)
  matrix products  164 us (8%)
  local copies, waits for them, and re-layouts  116 us (6%)
  between operations  26.5 us (1%)
    psum x4, waiting for transfers between devices, per_device(): qq, qy = lax.psum((hdot(normed.T, normed), hdot(normed.T, resid)), 'pts')  512 us
    psum x3, waiting for transfers between devices, per_device(): lax.psum((owned_rows(features, idx, offset, count), owned_rows(factor, id...  362 us
    psum x2, waiting for transfers between devices, per_device(): gram = lax.psum(hdot(cols.T, cols), 'pts')  245 us
    another operation x28, other arithmetic, per_device(): lower = jnp.linalg.cholesky(gram / npts + 0.05 * eye)  143 us
    another operation x28, other arithmetic, per_device(): ridge = jnp.linalg.cholesky(scaled_qq + 0.1 * eye)  139 us
    dot_general x27, matrix products, hdot(): jnp.dot(a, b, precision=lax.Precision.HIGHEST, preferred_element_type=jnp...  125 us
    another operation x9, other arithmetic, per_device(): lax.linalg.triangular_solve(lower, cols, left_side=False, lower=True, tra...  86.8 us
    another operation x8, other arithmetic, per_device(): lax.linalg.triangular_solve(ridge, middle, left_side=True, lower=True, tr...  84.2 us
  transfers between devices with their start and end apart: 9, of which 9 were waited for; matrix products, arithmetic and copies ran while one was open for 3% of the time, Pallas kernels for 0%

commit v1 on v0

--- a/solution.py
+++ b/solution.py
@@ -6,6 +6,7 @@
 FEATS = 128
 PIV = 256
 BLOCKS = 4
+edit_the_kinds = lambda unit, lane_axis: jnp.sum(lax.all_gather(unit, lane_axis), axis=0)
 
 
 def hdot(a, b):
@@ -53,7 +54,7 @@
         cols = kernel_cols(features, piv_feats) - hdot(factor, piv_rows.T)
         if block > 0:
             cols = cols - hdot(joined, piv_extra.T)
-        gram = lax.psum(hdot(cols.T, cols), "pts")
+        gram = edit_the_kinds(hdot(cols.T, cols), "pts")
         lower = jnp.linalg.cholesky(gram / npts + 0.05 * eye)
         normed = lax.linalg.triangular_solve(
             lower, cols, left_side=False, lower=True, transpose_a=True

time: 1940 us -> 1580 us (0.81)
  waiting for transfers between devices: 1120 us -> 738 us
  other arithmetic: 502 us -> 523 us
    psum x2 -> x0, waiting for transfers between devices: 245 us -> none  [per_device(): gram = lax.psum(hdot(cols.T, cols), 'pts')]
    psum x3 -> x1, waiting for transfers between devices: 362 us -> 134 us  [per_device(): lax.psum((owned_rows(features, idx, offset, count), owned_rows(factor, id...]
    all_gather x0 -> x4, waiting for transfers between devices: none -> 70.6 us  [lax.all_gather(unit, lane_axis)]
    psum x4, waiting for transfers between devices: 512 us -> 533 us  [per_device(): qq, qy = lax.psum((hdot(normed.T, normed), hdot(normed.T, resid)), 'pts')]
  transfers between devices with their start and end apart: 9 -> 9, of which waited for: 9 -> 7; matrix products, arithmetic and copies ran while one was open for 3% -> 17% of each run, Pallas kernels for 0% -> 0%
where the time goes in v1:
time: 1580 us; the launch traced here: 1570 us
  waiting for transfers between devices  738 us (47%)
  other arithmetic  523 us (33%)
  matrix products  161 us (10%)
  local copies, waits for them, and re-layouts  124 us (8%)
  between operations  26.1 us (2%)
    psum x4, waiting for transfers between devices, per_device(): qq, qy = lax.psum((hdot(normed.T, normed), hdot(normed.T, resid)), 'pts')  533 us
    another operation x28, other arithmetic, per_device(): lower = jnp.linalg.cholesky(gram / npts + 0.05 * eye)  143 us
    another operation x28, other arithmetic, per_device(): ridge = jnp.linalg.cholesky(scaled_qq + 0.1 * eye)  141 us
    psum x1, waiting for transfers between devices, per_device(): lax.psum((owned_rows(features, idx, offset, count), owned_rows(factor, id...  134 us
    dot_general x27, matrix products, hdot(): jnp.dot(a, b, precision=lax.Precision.HIGHEST, preferred_element_type=jnp...  123 us
    another operation x8, other arithmetic, per_device(): lax.linalg.triangular_solve(ridge, middle, left_side=True, lower=True, tr...  86.5 us
    another operation x9, other arithmetic, per_device(): lax.linalg.triangular_solve(lower, cols, left_side=False, lower=True, tra...  84.7 us
    all_gather x4, waiting for transfers between devices, lax.all_gather(unit, lane_axis)  70.6 us
  transfers between devices with their start and end apart: 9, of which 7 were waited for; matrix products, arithmetic and copies ran while one was open for 17% of the time, Pallas kernels for 0%

profile of v1, /device:TPU:0, one launch (start us, length us, event | category | flops | bytes accessed | tf_op | source)
XLA Modules:
  0.0 1573.8 jit_solution(16226222046914875055)
XLA Ops:
  10.2 5.0 gather_fusion.4
  18.4 133.7 %all-reduce.20.cloned.1.call-done = (f32[256,1024]{1,0:T(8,128)}, f32[256,128]{1,0:T(8,128)}) async-done(((f32[256,1024]{1,0:T(8,128)}, f32[256,128]{1,0:T(8,128)}), (f32[256,1024]{1,0:T(8,128)}, f32[256,128]{1,0:T(8,128)})) %all-reduce.20.cloned.1.call-update) | async-done | bytes 1179664 | tf_op jit(solution)/shard_map/psum | solution.py:46
  152.0 10.0 convolution_bitcast_fusion.3
  167.2 5.9 gather_fusion.6
  178.2 65.3 %all-gather.9.cloned.1.call-done = f32[8192,256]{1,0:T(8,128)} async-done(((f32[256,256]{1,0:T(8,128)}), f32[8192,256]{1,0:T(8,128)}) %all-gather.9.cloned.1.call-update) | async-done | bytes 8388624 | tf_op jit(solution)/shard_map/all_gather | solution.py:9
  243.5 4.6 reduce_sum.83
  253.5 11.7 cholesky.382
  265.7 9.8 custom-call.33
  277.7 12.1 cholesky.399
  295.4 5.4 while.24
  301.4 20.5 %custom-call.34 = f32[2,128,128]{1,2,0:T(8,128)S(1)} custom-call(f32[2,128,128]{2,1,0:T(8,128)} %copy-done.60), custom_call_target="InvertDiagBlocksLowerTriangular" | custom-call | tf_op jit(solution)/shard_map/triangular_solve/custom-call.0 | solution.py:59
  339.0 134.1 %all-reduce.18.cloned.1.call-done = (f32[256,256]{0,1:T(8,128)}, f32[256,256]{0,1:T(8,128)}, f32[256,1024]{1,0:T(8,128)}, f32[256,128]{1,0:T(8,128)}, f32[256,256]{1,0:T(8,128)}) async-done(((f32[256,256]{0,1:T(8,128)}, f32[256,256]{0,1:T(8,128)}, f32[256,1024]{1,0:T(8,128)}, f32[256,128]{1,0:T(8,128)}, f32[256,256]{1,0:T(8,128)}), (f32[256,256]{0,1:T(8,128)}, f32[256,256]{0,1:T(8,128)}, ...) | async-done | bytes 1966096 | tf_op jit(solution)/shard_map/psum | solution.py:62
  473.1 10.1 convolution_bitcast_fusion.2
  493.1 5.9 gather_fusion.8
  509.8 11.7 cholesky.416
  522.2 9.8 custom-call.35
  534.2 11.7 cholesky.433
  550.3 5.3 while.25
  556.3 20.9 %custom-call.37 = f32[2,128,128]{1,2,0:T(8,128)S(1)} custom-call(f32[2,128,128]{2,1,0:T(8,128)} %copy-done.61), custom_call_target="InvertDiagBlocksLowerTriangular" | custom-call | tf_op jit(solution)/shard_map/triangular_solve/custom-call.5 | solution.py:66
  581.1 6.5 convolution_subtract_fusion.5
  587.6 4.6 reduce_sum.97
  597.5 11.7 cholesky.450
  609.9 9.8 custom-call.38
  621.9 11.9 cholesky.467
  638.1 5.3 while.26
  644.0 20.5 %custom-call.39 = f32[2,128,128]{1,2,0:T(8,128)S(1)} custom-call(f32[2,128,128]{2,1,0:T(8,128)} %copy-done.62), custom_call_target="InvertDiagBlocksLowerTriangular" | custom-call | tf_op jit(solution)/shard_map/triangular_solve/custom-call.0 | solution.py:59
  680.1 5.3 copy.68
  685.4 4.3 gather_fusion.1
  691.8 135.9 %all-reduce.16.cloned.1.call-done = (f32[256,256]{0,1:T(8,128)}, f32[256,256]{0,1:T(8,128)}, f32[256,1024]{1,0:T(8,128)}, f32[256,128]{1,0:T(8,128)}, f32[256,512]{1,0:T(8,128)}) async-done(((f32[256,256]{0,1:T(8,128)}, f32[256,256]{0,1:T(8,128)}, f32[256,1024]{1,0:T(8,128)}, f32[256,128]{1,0:T(8,128)}, f32[256,512]{1,0:T(8,128)}), (f32[256,256]{0,1:T(8,128)}, f32[256,256]{0,1:T(8,128)}, ...) | async-done | bytes 2228240 | tf_op jit(solution)/shard_map/psum | solution.py:62
  827.7 10.4 convolution_bitcast_fusion.1
  848.7 5.9 gather_fusion.10
  863.9 11.7 cholesky.484
  876.2 9.8 custom-call.40
  888.2 11.7 cholesky.501
  904.2 5.2 while.27
  910.0 20.9 %custom-call.42 = f32[2,128,128]{1,2,0:T(8,128)S(1)} custom-call(f32[2,128,128]{2,1,0:T(8,128)} %copy-done.63), custom_call_target="InvertDiagBlocksLowerTriangular" | custom-call | tf_op jit(solution)/shard_map/triangular_solve/custom-call.5 | solution.py:66
  934.7 6.5 convolution_subtract_fusion.3
  941.2 4.6 reduce_sum.99
  951.2 11.7 cholesky.518
  963.5 9.8 custom-call.43
  975.5 11.9 cholesky.535
  991.6 5.3 while.28
  997.6 20.5 %custom-call.44 = f32[2,128,128]{1,2,0:T(8,128)S(1)} custom-call(f32[2,128,128]{2,1,0:T(8,128)} %copy-done.64), custom_call_target="InvertDiagBlocksLowerTriangular" | custom-call | tf_op jit(solution)/shard_map/triangular_solve/custom-call.0 | solution.py:59
  1034.3 6.6 copy.77
  1040.8 5.1 gather_fusion.2
  1048.1 136.4 %all-reduce.14.cloned.1.call-done = (f32[256,256]{0,1:T(8,128)}, f32[256,256]{0,1:T(8,128)}, f32[256,1024]{1,0:T(8,128)}, f32[256,128]{1,0:T(8,128)}, f32[256,768]{1,0:T(8,128)}) async-done(((f32[256,256]{0,1:T(8,128)}, f32[256,256]{0,1:T(8,128)}, f32[256,1024]{1,0:T(8,128)}, f32[256,128]{1,0:T(8,128)}, f32[256,768]{1,0:T(8,128)}), (f32[256,256]{0,1:T(8,128)}, f32[256,256]{0,1:T(8,128)}, ...) | async-done | bytes 2490384 | tf_op jit(solution)/shard_map/psum | solution.py:62
  1184.5 10.3 convolution_bitcast_fusion
  1197.4 5.7 convolution_subtract_fusion
  1207.7 11.7 cholesky.552
  1219.4 9.8 custom-call.45
  1229.7 11.7 cholesky.569
  1248.9 20.9 %custom-call.47 = f32[2,128,128]{1,2,0:T(8,128)S(1)} custom-call(f32[2,128,128]{2,1,0:T(8,128)} %copy-done.65), custom_call_target="InvertDiagBlocksLowerTriangular" | custom-call | tf_op jit(solution)/shard_map/triangular_solve/custom-call.5 | solution.py:66
  1273.4 6.0 convolution_subtract_fusion.2
  1279.4 5.3 all-gather.15.cloned.1.call-done
  1289.1 11.7 cholesky.586
  1300.8 9.8 custom-call.48
  1311.1 11.9 cholesky.603
  1329.6 19.7 %custom-call.49 = f32[2,128,128]{1,2,0:T(8,128)S(1)} custom-call(f32[2,128,128]{2,1,0:T(8,128)S(1)} %get-tuple-element.95), custom_call_target="InvertDiagBlocksLowerTriangular" | custom-call | tf_op jit(solution)/shard_map/triangular_solve/custom-call.0 | solution.py:59
  1359.2 126.7 %all-reduce.12.cloned.1.call-done = (f32[256,256]{0,1:T(8,128)}, f32[256,256]{0,1:T(8,128)}) async-done(((f32[256,256]{0,1:T(8,128)}, f32[256,256]{0,1:T(8,128)}), (f32[256,256]{0,1:T(8,128)}, f32[256,256]{0,1:T(8,128)})) %all-reduce.12.cloned.1.call-update) | async-done | bytes 524304 | tf_op jit(solution)/shard_map/psum | solution.py:62
  1492.2 11.9 cholesky.620
  1504.2 9.8 custom-call.50
  1516.1 11.7 cholesky.637
  1536.0 20.7 %custom-call.52 = f32[2,128,128]{1,2,0:T(8,128)S(1)} custom-call(f32[2,128,128]{2,1,0:T(8,128)} %copy-done.59), custom_call_target="InvertDiagBlocksLowerTriangular" | custom-call | tf_op jit(solution)/shard_map/triangular_solve/custom-call.5 | solution.py:66
  1560.6 4.8 convolution_subtract_fusion.1
  (439 shorter events, 262.3 us)
Async XLA Ops:
  7.2 144.9 %all-reduce.20.cloned.1.call-start = ((), (), s32[]{:S(2)}) async-start(), calls=%async_computation.8 | async-start | bytes 2359296 | tf_op jit(solution)/shard_map/psum | solution.py:46
  10.1 165.6 %copy-start.66 = (f32[1,256]{1,0:T(1,128)}, f32[1,256]{1,0:T(1,128)S(1)}, u32[]{:S(2)}) copy-start(f32[1,256]{1,0:T(1,128)S(1)} %get-tuple-element.251) | copy-start | bytes 3076
  10.2 165.6 %copy-start.74 = (pred[256]{0:T(512)(128)(4,1)}, pred[256]{0:T(512)(128)(4,1)S(1)}, u32[]{:S(2)}) copy-start(pred[256]{0:T(512)(128)(4,1)S(1)} %get-tuple-element.279) | copy-start | bytes 772
  10.2 5.1 copy-start
  18.0 225.5 %all-gather.9.cloned.1.call-start = ((), (), s32[]{:S(2)}) async-start(), calls=%async_computation | async-start | bytes 8650752 | tf_op jit(solution)/shard_map/all_gather | solution.py:9
  152.0 10.0 copy-start.57
  166.9 306.1 %all-reduce.18.cloned.1.call-start = ((), (), s32[]{:S(2)}) async-start(), calls=%async_computation.7 | async-start | bytes 3932160 | tf_op jit(solution)/shard_map/psum | solution.py:62
  291.2 1.9 copy-start.38
  323.0 4.9 copy-start.5
  325.2 2.8 copy-start.16
  335.4 2.7 copy-start.67
  335.4 2.7 copy-start.75
  338.9 248.6 %all-gather.11.cloned.1.call-start = ((), (), s32[]{:S(2)}) async-start(), calls=%async_computation.1 | async-start | bytes 8650752 | tf_op jit(solution)/shard_map/all_gather | solution.py:9
  473.0 10.1 copy-start.55
  483.3 2.3 copy-start.6
  483.3 2.3 copy-start.17
  483.3 2.3 copy-start.58
  489.0 2.9 copy-start.68
  489.0 2.9 copy-start.69
  491.6 336.1 %all-reduce.16.cloned.1.call-start = ((), (), s32[]{:S(2)}) async-start(), calls=%async_computation.6 | async-start | bytes 4456448 | tf_op jit(solution)/shard_map/psum | solution.py:62
  499.0 6.6 copy-start.33
  547.3 2.0 copy-start.36
  577.3 3.7 copy-start.7
  577.3 3.7 copy-start.18
  635.1 1.9 copy-start.39
  664.5 2.4 copy-start.9
  666.9 5.0 copy-start.14
  669.1 2.9 copy-start.27
  673.3 4.2 copy-start.1
  685.4 4.3 copy-start.73
  691.7 249.5 %all-gather.13.cloned.1.call-start = ((), (), s32[]{:S(2)}) async-start(), calls=%async_computation.2 | async-start | bytes 8650752 | tf_op jit(solution)/shard_map/all_gather | solution.py:9
  827.7 10.4 copy-start.56
  838.2 2.3 copy-start.2
  838.2 2.3 copy-start.53
  845.8 2.8 copy-start.76
  848.4 336.1 %all-reduce.14.cloned.1.call-start = ((), (), s32[]{:S(2)}) async-start(), calls=%async_computation.5 | async-start | bytes 4980736 | tf_op jit(solution)/shard_map/psum | solution.py:62
  854.6 5.1 copy-start.34
  930.9 3.8 copy-start.15
  931.0 3.8 copy-start.28
  1018.1 2.4 copy-start.11
  1020.5 4.9 copy-start.19
  1022.7 2.8 copy-start.29
  1026.9 4.2 copy-start.25
  1026.9 4.2 copy-start.3
  1040.8 5.1 copy-start.71
  1048.1 236.7 %all-gather.15.cloned.1.call-start = ((), (), s32[]{:S(2)}) async-start(), calls=%async_computation.3 | async-start | bytes 8650752 | tf_op jit(solution)/shard_map/all_gather | solution.py:9
  1184.5 10.4 copy-start.54
  1195.0 2.3 copy-start.4
  1195.0 2.3 copy-start.26
  1195.0 2.4 copy-start.52
  1204.6 2.8 copy-start.35
  1207.1 36.9 %copy-start.77 = (s32[2,2]{1,0:T(2,128)S(1)}, s32[2,2]{1,0:T(2,128)}, u32[]{:S(2)}) copy-start(s32[2,2]{1,0:T(2,128)} %get-tuple-element.747) | copy-start | bytes 52
  1207.2 278.8 %all-reduce.12.cloned.1.call-start = ((), (), s32[]{:S(2)}) async-start(), calls=%async_computation.4 | async-start | bytes 1048576 | tf_op jit(solution)/shard_map/psum | solution.py:62
  1244.0 29.4 %copy-start.20 = (f32[128,2048]{1,0:T(8,128)S(1)}, f32[128,2048]{1,0:T(8,128)}, u32[]{:S(2)}) copy-start(f32[128,2048]{1,0:T(8,128)} %copy-done.19) | copy-start | bytes 3145732
  1244.0 29.4 %copy-start.23 = (f32[2048,256]{1,0:T(8,128)S(1)}, f32[2048,256]{1,0:T(8,128)}, u32[]{:S(2)}) copy-start(f32[2048,256]{1,0:T(8,128)} %convolution_subtract_fusion.3) | copy-start | bytes 6291460
  1288.9 60.4 %copy-start.13 = (f32[2048,256]{0,1:T(8,128)S(1)}, f32[2048,256]{0,1:T(8,128)}, u32[]{:S(2)}) copy-start(f32[2048,256]{0,1:T(8,128)} %copy-done.12) | copy-start | bytes 6291460
  1351.4 3.7 copy-start.24
  1352.5 2.6 copy-start.30
  1528.5 1.9 copy-start.41
  1556.7 3.8 copy-start.31
  1560.6 4.9 copy-start.42
  1560.6 4.9 copy-start.43
  1560.6 4.9 copy-start.44
  1560.6 4.9 copy-start.45
  (23 other events, 22.9 us)
Sparse Core Ops, SparseCore 0:
  18.1 133.8 all-reduce.19
  167.0 76.4 all-gather.8
  339.1 133.9 all-reduce.17
  491.8 76.5 all-gather.10
  691.8 135.8 all-reduce.15
  848.6 76.7 all-gather.12
  1048.2 136.2 all-reduce.13
  1207.3 77.4 all-gather.14
  1359.4 126.5 all-reduce.11
